TPU v7x, 32 devices: a whole 2x2x4 slice. The times are simulated.
32 devices in a mesh: domain: 8 (over z, y), vec: 4 (over x, core).
Axes of the slice: x: 2, y: 2, z: 4, core: 2. Of those that a mesh axis runs over, the one named last changes fastest.
Arguments:
- vectors: float32 [4096, 512], P('domain', 'vec'), may hold values from -6 to 6
- hamiltonian: float32 [512, 128, 128], P('domain'), may hold values from -0.09375 to 0.09375
- tile_pairs: int32 [512, 2], P('domain'), may hold values from 0 to 31, as said below
- tile_counts: int32 [8], P('domain'), may hold values from 8 to 64, as said below
Outputs:
- filtered: float32 [4096, 512], P('domain', 'vec')
- gram: float32 [512, 512], P('vec')
Inputs may be any that keep to these rules, and one draw needn't show every extreme that they name: `tile_pairs`: slots k * 64 to (k + 1) * 64 - 1 have their row group r among groups k * 4 to (k + 1) * 4 - 1 and their column group c with r <= c <= min(k * 4 + 3 * 4 - 1, 31); pairs may repeat, and repeated blocks add. `tile_counts`: one domain index uses all 64 slots.
All inputs are finite; a program needn't handle non-finite values.
Results may differ from a plain program's by a relative error of at most 0.0003.
Values sent between devices are 32-bit elements; how exact they have to be, the bound alone decides.
A program may use at most 64 MiB of HBM per device.

v0:
```python
import jax
import jax.numpy as jnp
from jax import lax
from jax.sharding import PartitionSpec as P

TILE = 128
REACH = 2
center_shift = 1.0
half_width = 1.5


def from_behind(block, axis, distance):
    devices = range(lax.axis_size(axis))
    route = [(i - distance, i) for i in devices if i - distance in devices]
    return lax.ppermute(block, axis, route)


def local_products(own, window, tiles, row_loc, col_loc, count, groups):
    block_slots = 8
    width = own.shape[2]
    span = window.shape[0]
    n_blocks = (count + block_slots - 1) // block_slots

    def block_step(index, carry):
        rows_acc, back_acc = carry
        start = index * block_slots
        tile = lax.dynamic_slice_in_dim(tiles, start, block_slots, 0)
        rloc = lax.dynamic_slice_in_dim(row_loc, start, block_slots, 0)
        cloc = lax.dynamic_slice_in_dim(col_loc, start, block_slots, 0)
        used = (start + jnp.arange(block_slots, dtype=jnp.int32) < count).astype(jnp.float32)
        apart = (rloc != cloc).astype(jnp.float32)
        fwd = jnp.einsum("tij,tjc->tic", tile, window[cloc], precision=lax.Precision.HIGHEST)
        back = jnp.einsum("tji,tjc->tic", tile, own[rloc], precision=lax.Precision.HIGHEST)
        row_hot = (rloc[:, None] == jnp.arange(groups, dtype=jnp.int32)[None, :]).astype(
            jnp.float32
        ) * used[:, None]
        col_hot = (cloc[:, None] == jnp.arange(span, dtype=jnp.int32)[None, :]).astype(
            jnp.float32
        ) * (used * apart)[:, None]
        rows_acc = rows_acc + jnp.einsum(
            "tg,tic->gic", row_hot, fwd, precision=lax.Precision.HIGHEST
        )
        back_acc = back_acc + jnp.einsum(
            "tg,tic->gic", col_hot, back, precision=lax.Precision.HIGHEST
        )
        return (rows_acc, back_acc)

    start_rows = jnp.zeros((groups, TILE, width), jnp.float32)
    start_back = jnp.zeros((span, TILE, width), jnp.float32)
    return lax.fori_loop(0, n_blocks, block_step, (start_rows, start_back))


def apply_ham(block, tiles, row_loc, col_loc, count):
    groups = block.shape[0] // TILE
    width = block.shape[1]
    own = block.reshape(groups, TILE, width)
    pieces = [own]
    for step in range(1, REACH + 1):
        pieces.append(from_behind(own, "domain", -step))
    window = jnp.concatenate(pieces, 0)
    rows_acc, back_acc = local_products(own, window, tiles, row_loc, col_loc, count, groups)
    result = rows_acc + back_acc[:groups]
    for step in range(1, REACH + 1):
        result = result + from_behind(back_acc[step * groups : (step + 1) * groups], "domain", step)
    return result.reshape(groups * TILE, width)


def shards(vectors, hamiltonian, tile_pairs, tile_counts):
    groups = vectors.shape[0] // TILE
    base = lax.axis_index("domain") * groups
    count = tile_counts[0]
    diag = tile_pairs[:, 0] == tile_pairs[:, 1]
    tiles = jnp.where(
        diag[:, None, None], 0.5 * (hamiltonian + jnp.swapaxes(hamiltonian, 1, 2)), hamiltonian
    )
    row_loc = tile_pairs[:, 0] - base
    col_loc = tile_pairs[:, 1] - base
    second = (
        apply_ham(vectors, tiles, row_loc, col_loc, count) - center_shift * vectors
    ) / half_width
    third = (
        2.0
        * (apply_ham(second, tiles, row_loc, col_loc, count) - center_shift * second)
        / half_width
        - vectors
    )
    filtered = (
        2.0 * (apply_ham(third, tiles, row_loc, col_loc, count) - center_shift * third) / half_width
        - second
    )
    total_rows = vectors.shape[0] * lax.axis_size("domain")
    gathered = lax.all_gather(filtered, "vec", axis=1, tiled=True)
    partial_block = (
        jnp.dot(
            filtered.T,
            gathered,
            precision=lax.Precision.HIGHEST,
            preferred_element_type=jnp.float32,
        )
        / total_rows
    )
    gram = lax.psum(partial_block, "domain")
    return (filtered, gram)


def solution(mesh):
    in_specs = (P("domain", "vec"), P("domain", None, None), P("domain", None), P("domain"))
    out_specs = (P("domain", "vec"), P("vec", None))
    return jax.shard_map(shards, mesh=mesh, in_specs=in_specs, out_specs=out_specs, check_vma=False)
```

profile of v0, /device:TPU:0, one launch (start us, length us, event | category | flops | bytes accessed | tf_op | source)
XLA Modules:
  0.0 392.4 jit_solution(13187985193437510828)
XLA Ops:
  9.8 5.6 %copy.6 = f32[64,128,128]{1,2,0:T(8,128)} copy(f32[64,128,128]{2,1,0:T(8,128)} %param.11) | data formatting | bytes 8388608 | tf_op args[1]
  15.4 5.9 %fusion.61 = f32[64,128,128]{2,1,0:T(8,128)} fusion(f32[64,128,128]{2,1,0:T(8,128)} %param.11, f32[64,128,128]{1,2,0:T(8,128)} %copy.6, pred[64]{0:T(512)(128)(4,1)S(1)} %compare_bitcast_fusion), kind=kLoop, calls=%fused_computation.98 | loop fusion | flops 3145728 | bytes 12582976 | tf_op jit(solution)/shard_map/jit(_where)/select_n | solution.py:73
  22.3 24.5 %while.36 = (s32[]{:T(128)}, f32[4,128,128]{2,0,1:T(4,128)S(1)}, f32[12,128,128]{2,0,1:T(8,128)S(1)}, s32[]{:T(128)}, s32[64]{0:T(128)S(1)}, /*index=5*/s32[]{:T...) while((s32[]{:T(128)}, f32[4,128,128]{2,0,1:T(4,128)S(1)}, ...), condition=%wide.region_1.2_spmd, body=%wide.region_0.1_spmd.sunk | while | flops 428083552 | bytes 8397583 | solution.py:50
  23.6 1.7 fusion.116
  26.9 2.1 fusion.117
  29.0 1.5 convolution_add_fusion.13
  31.8 1.7 fusion.116
  35.1 2.1 fusion.117
  37.1 1.5 convolution_add_fusion.13
  40.0 1.7 fusion.116
  43.2 2.1 fusion.117
  45.3 1.5 convolution_add_fusion.13
  46.9 1.3 collective-permute-start.3
  48.2 5.6 %collective-permute-start.2 = (f32[4,128,128]{2,0,1:T(4,128)S(1)}, f32[4,128,128]{2,0,1:T(4,128)S(1)}, u32[]{:S(2)}, u32[]{:S(2)}) collective-permute-start(f32[4,128,128]{2,0,1:T(4,128)S(1)} %get-tuple-element.252), channel_id=1, source_target_pairs={{0,4},{4,8},{8,12},{12,16},{16,20},{20,24},{24,28},{1,5},{5,9},{9,... | collective-permute-start | bytes 786440 | tf_op jit(solution)/shard_map/ppermute | solution.py:15
  54.7 4.6 %collective-permute-done.2 = f32[4,128,128]{2,0,1:T(4,128)S(1)} collective-permute-done((f32[4,128,128]{2,0,1:T(4,128)S(1)}, f32[4,128,128]{2,0,1:T(4,128)S(1)}, u32[]{:S(2)}, u32[]{:S(2)}) %collective-permute-start.2) | collective-permute-done | bytes 262176 | tf_op jit(solution)/shard_map/ppermute | solution.py:15
  59.5 1.3 collective-permute-start.5
  62.1 51.8 %collective-permute-done.5 = f32[4,128,128]{2,1,0:T(8,128)S(1)} collective-permute-done((f32[4,128,128]{2,1,0:T(8,128)S(1)}, f32[4,128,128]{2,1,0:T(8,128)S(1)}, u32[]{:S(2)}, u32[]{:S(2)}) %collective-permute-start.5) | collective-permute-done | bytes 262176 | tf_op jit(solution)/shard_map/ppermute | solution.py:15
  114.1 24.5 %while.37 = (s32[]{:T(128)}, f32[4,128,128]{2,0,1:T(4,128)S(1)}, f32[12,128,128]{2,0,1:T(8,128)S(1)}, s32[]{:T(128)}, s32[64]{0:T(128)S(1)}, /*index=5*/s32[]{:T...) while((s32[]{:T(128)}, f32[4,128,128]{2,0,1:T(4,128)S(1)}, ...), condition=%wide.region_3.4_spmd, body=%wide.region_2.3_spmd.sunk | while | flops 428083552 | bytes 8397583 | solution.py:50
  115.4 1.7 fusion.126
  118.7 2.1 fusion.127
  120.8 1.5 convolution_add_fusion.15
  123.6 1.7 fusion.126
  126.9 2.1 fusion.127
  128.9 1.5 convolution_add_fusion.15
  131.8 1.7 fusion.126
  135.0 2.1 fusion.127
  137.1 1.5 convolution_add_fusion.15
  138.7 1.3 collective-permute-start.7
  140.0 6.4 %collective-permute-start.6 = (f32[4,128,128]{2,0,1:T(4,128)S(1)}, f32[4,128,128]{2,0,1:T(4,128)S(1)}, u32[]{:S(2)}, u32[]{:S(2)}) collective-permute-start(f32[4,128,128]{2,0,1:T(4,128)S(1)} %get-tuple-element.250), channel_id=1, source_target_pairs={{0,4},{4,8},{8,12},{12,16},{16,20},{20,24},{24,28},{1,5},{5,9},{9,... | collective-permute-start | bytes 786440 | tf_op jit(solution)/shard_map/ppermute | solution.py:15
  146.5 3.8 collective-permute-done.6
  153.2 54.4 %collective-permute-done.9 = f32[4,128,128]{2,1,0:T(8,128)S(1)} collective-permute-done((f32[4,128,128]{2,1,0:T(8,128)S(1)}, f32[4,128,128]{2,1,0:T(8,128)S(1)}, u32[]{:S(2)}, u32[]{:S(2)}) %collective-permute-start.9) | collective-permute-done | bytes 262176 | tf_op jit(solution)/shard_map/ppermute | solution.py:15
  207.7 24.7 %while.38 = (s32[]{:T(128)}, f32[4,128,128]{2,0,1:T(4,128)S(1)}, f32[12,128,128]{2,0,1:T(8,128)S(1)}, s32[]{:T(128)}, s32[64]{0:T(128)S(1)}, /*index=5*/s32[]{:T...) while((s32[]{:T(128)}, f32[4,128,128]{2,0,1:T(4,128)S(1)}, ...), condition=%wide.region_5.6_spmd, body=%wide.region_4.5_spmd.sunk | while | flops 428083552 | bytes 8397583 | solution.py:50
  209.3 1.7 fusion.136
  212.5 2.1 fusion.137
  214.6 1.5 convolution_add_fusion.17
  217.4 1.7 fusion.136
  220.7 2.1 fusion.137
  222.8 1.5 convolution_add_fusion.17
  225.6 1.7 fusion.136
  228.9 2.1 fusion.137
  230.9 1.5 convolution_add_fusion.17
  232.5 1.3 collective-permute-start.11
  233.9 6.2 %collective-permute-start.10 = (f32[4,128,128]{2,0,1:T(4,128)S(1)}, f32[4,128,128]{2,0,1:T(4,128)S(1)}, u32[]{:S(2)}, u32[]{:S(2)}) collective-permute-start(f32[4,128,128]{2,0,1:T(4,128)S(1)} %get-tuple-element.248), channel_id=1, source_target_pairs={{0,4},{4,8},{8,12},{12,16},{16,20},{20,24},{24,28},{1,5},{5,9},{9,... | collective-permute-start | bytes 786440 | tf_op jit(solution)/shard_map/ppermute | solution.py:15
  240.1 3.8 collective-permute-done.10
  244.9 64.1 %all-gather.2.cloned.1.call-done = f32[512,512]{1,0:T(8,128)} async-done(((f32[512,128]{1,0:T(8,128)}), f32[512,512]{1,0:T(8,128)}) %all-gather.2.cloned.1.call-update) | async-done | bytes 1048592 | tf_op jit(solution)/shard_map/all_gather | solution.py:92
  308.9 2.8 convolution_multiply_fusion
  311.7 72.2 %all-reduce.2.cloned.1.call-done = f32[128,512]{1,0:T(8,128)} async-done(((f32[128,512]{1,0:T(8,128)}), f32[128,512]{1,0:T(8,128)}) %all-reduce.2.cloned.1.call-update) | async-done | bytes 262160 | tf_op jit(solution)/shard_map/psum | solution.py:102
  383.9 1.7 copy.69
  (106 shorter events, 35.2 us)
Async XLA Ops:
  7.2 301.8 %all-gather.2.cloned.1.call-start = ((), (), s32[]{:S(2)}) async-start(), calls=%async_computation | async-start | bytes 1310720 | tf_op jit(solution)/shard_map/all_gather | solution.py:92
  7.2 8.2 %copy-start.1 = (s32[64,2]{0,1:T(2,128)S(1)}, s32[64,2]{0,1:T(2,128)}, u32[]{:S(2)}) copy-start(s32[64,2]{0,1:T(2,128)} %param.12) | copy-start | bytes 1540
  7.2 14.9 %collective-permute-start.1 = (f32[4,128,128]{2,1,0:T(8,128)}, f32[4,128,128]{2,1,0:T(8,128)S(1)}, u32[]{:S(2)}, u32[]{:S(2)}) collective-permute-start(f32[4,128,128]{2,1,0:T(8,128)} %bitcast.89), channel_id=1, source_target_pairs={{8,0},{12,4},{16,8},{20,12},{24,16},{28,20},{9,1},{13,5},{17,9},{2... | collective-permute-start | bytes 786440 | tf_op jit(solution)/shard_map/ppermute | solution.py:15
  8.5 13.6 %collective-permute-start = (f32[4,128,128]{2,1,0:T(8,128)}, f32[4,128,128]{2,1,0:T(8,128)S(1)}, u32[]{:S(2)}, u32[]{:S(2)}) collective-permute-start(f32[4,128,128]{2,1,0:T(8,128)} %bitcast.90), channel_id=1, source_target_pairs={{4,0},{8,4},{12,8},{16,12},{20,16},{24,20},{28,24},{5,1},{9,5},{13... | collective-permute-start | bytes 786440 | tf_op jit(solution)/shard_map/ppermute | solution.py:15
  15.4 6.7 %copy-start = (f32[512,128]{1,0:T(8,128)S(1)}, f32[512,128]{1,0:T(8,128)}, u32[]{:S(2)}) copy-start(f32[512,128]{1,0:T(8,128)} %param.10) | copy-start | bytes 786436
  46.9 7.8 %collective-permute-start.3 = (f32[4,128,128]{2,0,1:T(4,128)S(1)}, f32[4,128,128]{2,0,1:T(4,128)S(1)}, u32[]{:S(2)}, u32[]{:S(2)}) collective-permute-start(f32[4,128,128]{2,0,1:T(4,128)S(1)} %get-tuple-element.253), channel_id=1, source_target_pairs={{0,8},{4,12},{8,16},{12,20},{16,24},{20,28},{1,9},{5,13},{9,17},{1... | collective-permute-start | bytes 786440 | tf_op jit(solution)/shard_map/ppermute | solution.py:15
  48.2 11.1 %collective-permute-start.2 = (f32[4,128,128]{2,0,1:T(4,128)S(1)}, f32[4,128,128]{2,0,1:T(4,128)S(1)}, u32[]{:S(2)}, u32[]{:S(2)}) collective-permute-start(f32[4,128,128]{2,0,1:T(4,128)S(1)} %get-tuple-element.252), channel_id=1, source_target_pairs={{0,4},{4,8},{8,12},{12,16},{16,20},{20,24},{24,28},{1,5},{5,9},{9,... | collective-permute-start | bytes 786440 | tf_op jit(solution)/shard_map/ppermute | solution.py:15
  59.5 54.4 %collective-permute-start.5 = (f32[4,128,128]{2,1,0:T(8,128)S(1)}, f32[4,128,128]{2,1,0:T(8,128)S(1)}, u32[]{:S(2)}, u32[]{:S(2)}) collective-permute-start(f32[4,128,128]{2,1,0:T(8,128)S(1)} %bitcast.83), channel_id=1, source_target_pairs={{8,0},{12,4},{16,8},{20,12},{24,16},{28,20},{9,1},{13,5},{17,9},{2... | collective-permute-start | bytes 786440 | tf_op jit(solution)/shard_map/ppermute | solution.py:15
  60.8 53.1 %collective-permute-start.4 = (f32[4,128,128]{2,1,0:T(8,128)S(1)}, f32[4,128,128]{2,1,0:T(8,128)S(1)}, u32[]{:S(2)}, u32[]{:S(2)}) collective-permute-start(f32[4,128,128]{2,1,0:T(8,128)S(1)} %bitcast.84), channel_id=1, source_target_pairs={{4,0},{8,4},{12,8},{16,12},{20,16},{24,20},{28,24},{5,1},{9,5},{13... | collective-permute-start | bytes 786440 | tf_op jit(solution)/shard_map/ppermute | solution.py:15
  138.7 7.8 %collective-permute-start.7 = (f32[4,128,128]{2,0,1:T(4,128)S(1)}, f32[4,128,128]{2,0,1:T(4,128)S(1)}, u32[]{:S(2)}, u32[]{:S(2)}) collective-permute-start(f32[4,128,128]{2,0,1:T(4,128)S(1)} %get-tuple-element.251), channel_id=1, source_target_pairs={{0,8},{4,12},{8,16},{12,20},{16,24},{20,28},{1,9},{5,13},{9,17},{1... | collective-permute-start | bytes 786440 | tf_op jit(solution)/shard_map/ppermute | solution.py:15
  140.0 10.3 %collective-permute-start.6 = (f32[4,128,128]{2,0,1:T(4,128)S(1)}, f32[4,128,128]{2,0,1:T(4,128)S(1)}, u32[]{:S(2)}, u32[]{:S(2)}) collective-permute-start(f32[4,128,128]{2,0,1:T(4,128)S(1)} %get-tuple-element.250), channel_id=1, source_target_pairs={{0,4},{4,8},{8,12},{12,16},{16,20},{20,24},{24,28},{1,5},{5,9},{9,... | collective-permute-start | bytes 786440 | tf_op jit(solution)/shard_map/ppermute | solution.py:15
  150.6 57.0 %collective-permute-start.9 = (f32[4,128,128]{2,1,0:T(8,128)S(1)}, f32[4,128,128]{2,1,0:T(8,128)S(1)}, u32[]{:S(2)}, u32[]{:S(2)}) collective-permute-start(f32[4,128,128]{2,1,0:T(8,128)S(1)} %bitcast.95), channel_id=1, source_target_pairs={{8,0},{12,4},{16,8},{20,12},{24,16},{28,20},{9,1},{13,5},{17,9},{2... | collective-permute-start | bytes 786440 | tf_op jit(solution)/shard_map/ppermute | solution.py:15
  151.9 55.7 %collective-permute-start.8 = (f32[4,128,128]{2,1,0:T(8,128)S(1)}, f32[4,128,128]{2,1,0:T(8,128)S(1)}, u32[]{:S(2)}, u32[]{:S(2)}) collective-permute-start(f32[4,128,128]{2,1,0:T(8,128)S(1)} %bitcast.96), channel_id=1, source_target_pairs={{4,0},{8,4},{12,8},{16,12},{20,16},{24,20},{28,24},{5,1},{9,5},{13... | collective-permute-start | bytes 786440 | tf_op jit(solution)/shard_map/ppermute | solution.py:15
  232.5 7.5 %collective-permute-start.11 = (f32[4,128,128]{2,0,1:T(4,128)S(1)}, f32[4,128,128]{2,0,1:T(4,128)S(1)}, u32[]{:S(2)}, u32[]{:S(2)}) collective-permute-start(f32[4,128,128]{2,0,1:T(4,128)S(1)} %get-tuple-element.249), channel_id=1, source_target_pairs={{0,8},{4,12},{8,16},{12,20},{16,24},{20,28},{1,9},{5,13},{9,17},{1... | collective-permute-start | bytes 786440 | tf_op jit(solution)/shard_map/ppermute | solution.py:15
  233.9 10.1 %collective-permute-start.10 = (f32[4,128,128]{2,0,1:T(4,128)S(1)}, f32[4,128,128]{2,0,1:T(4,128)S(1)}, u32[]{:S(2)}, u32[]{:S(2)}) collective-permute-start(f32[4,128,128]{2,0,1:T(4,128)S(1)} %get-tuple-element.248), channel_id=1, source_target_pairs={{0,4},{4,8},{8,12},{12,16},{16,20},{20,24},{24,28},{1,5},{5,9},{9,... | collective-permute-start | bytes 786440 | tf_op jit(solution)/shard_map/ppermute | solution.py:15
  244.8 139.1 %all-reduce.2.cloned.1.call-start = ((), (), s32[]{:S(2)}) async-start(), calls=%async_computation.1 | async-start | bytes 524288 | tf_op jit(solution)/shard_map/psum | solution.py:102
Sparse Core Ops, SparseCore 0:
  244.9 63.9 all-gather.1
  312.8 71.0 all-reduce.1
where the time goes:
time: 395 us; the launch traced here: 392 us
  waiting for transfers between devices  256 us (65%)
  matrix products  58.6 us (15%)
  starting transfers between devices  30 us (8%)
  local copies, waits for them, and re-layouts  18.4 us (5%)
  between operations  15 us (4%)
  other arithmetic  14 us (4%)
    ppermute x12, waiting for transfers between devices, from_behind(): return lax.ppermute(block, axis, route)  119 us
    psum x1, waiting for transfers between devices, shards(): gram = lax.psum(partial_block, 'domain')  72.2 us
    all_gather x1, waiting for transfers between devices, shards(): gathered = lax.all_gather(filtered, 'vec', axis=1, tiled=True)  64.1 us
    ppermute x12, starting transfers between devices, from_behind(): return lax.ppermute(block, axis, route)  29.9 us
    dot_general x9, matrix products, block_step(): jnp.einsum('tji,tjc->tic', tile, own[rloc], precision=lax.Precision.HIGHEST)  18.5 us
    dot_general x9, matrix products, block_step(): jnp.einsum('tij,tjc->tic', tile, window[cloc], precision=lax.Precision.HI...  15.2 us
    dot_general x9, matrix products, block_step(): jnp.einsum('tg,tic->gic', col_hot, back, precision=lax.Precision.HIGHEST)  13.5 us
    dot_general x9, matrix products, block_step(): jnp.einsum('tg,tic->gic', row_hot, fwd, precision=lax.Precision.HIGHEST)  8.57 us
  transfers between devices with their start and end apart: 14, of which 8 were waited for; matrix products, arithmetic and copies ran while one was open for 3% of the time, Pallas kernels for 0%

commit v1 on v0

--- a/solution.py
+++ b/solution.py
@@ -1,3 +1,4 @@
+import functools
 import jax
 import jax.numpy as jnp
 from jax import lax
@@ -7,6 +8,24 @@
 REACH = 2
 center_shift = 1.0
 half_width = 1.5
+
+
+def run_joints(unit, chip_axis):
+    n_peers_all = lax.axis_size(chip_axis)
+    ready, n_now = (unit, 0)
+    while 1 << n_now < n_peers_all:
+        xs_all = []
+        ii = 0
+        while ii < n_peers_all:
+            xs_all.append((ii, ii ^ 1 << n_now))
+            ii += 1
+        big = lax.ppermute(ready, axis_name=chip_axis, perm=xs_all)
+        ready = ready + big
+        n_now = n_now + 1
+    return ready
+
+
+_time_halves = functools.partial(run_joints, chip_axis="domain")
 
 
 def from_behind(block, axis, distance):
@@ -99,7 +118,7 @@
         )
         / total_rows
     )
-    gram = lax.psum(partial_block, "domain")
+    gram = _time_halves(partial_block)
     return (filtered, gram)
 
 

time: 395 us -> 351 us (0.89)
  waiting for transfers between devices: 256 us -> 207 us
  starting transfers between devices: 30 us -> 35.5 us
    psum x1 -> x0, waiting for transfers between devices: 72.2 us -> none  [shards(): gram = lax.psum(partial_block, 'domain')]
    ppermute x0 -> x3, waiting for transfers between devices: none -> 23.9 us  [run_joints(): big = lax.ppermute(ready, axis_name=chip_axis, perm=xs_all)]
    ppermute x0 -> x3, starting transfers between devices: none -> 5.56 us  [run_joints(): big = lax.ppermute(ready, axis_name=chip_axis, perm=xs_all)]
  transfers between devices with their start and end apart: 14 -> 16, of which waited for: 8 -> 10; matrix products, arithmetic and copies ran while one was open for 3% -> 3% of each run, Pallas kernels for 0% -> 0%
where the time goes in v1:
time: 351 us; the launch traced here: 348 us
  waiting for transfers between devices  207 us (59%)
  matrix products  57.9 us (16%)
  starting transfers between devices  35.5 us (10%)
  local copies, waits for them, and re-layouts  16.8 us (5%)
  between operations  15 us (4%)
  other arithmetic  14.8 us (4%)
    ppermute x12, waiting for transfers between devices, from_behind(): return lax.ppermute(block, axis, route)  119 us
    all_gather x1, waiting for transfers between devices, shards(): gathered = lax.all_gather(filtered, 'vec', axis=1, tiled=True)  64.1 us
    ppermute x12, starting transfers between devices, from_behind(): return lax.ppermute(block, axis, route)  29.9 us
    ppermute x3, waiting for transfers between devices, run_joints(): big = lax.ppermute(ready, axis_name=chip_axis, perm=xs_all)  23.9 us
    dot_general x9, matrix products, block_step(): jnp.einsum('tji,tjc->tic', tile, own[rloc], precision=lax.Precision.HIGHEST)  18.5 us
    dot_general x9, matrix products, block_step(): jnp.einsum('tij,tjc->tic', tile, window[cloc], precision=lax.Precision.HI...  15.2 us
    dot_general x9, matrix products, block_step(): jnp.einsum('tg,tic->gic', col_hot, back, precision=lax.Precision.HIGHEST)  13.5 us
    dot_general x9, matrix products, block_step(): jnp.einsum('tg,tic->gic', row_hot, fwd, precision=lax.Precision.HIGHEST)  8.57 us
  transfers between devices with their start and end apart: 16, of which 10 were waited for; matrix products, arithmetic and copies ran while one was open for 3% of the time, Pallas kernels for 0%

profile of v1, /device:TPU:0, one launch (start us, length us, event | category | flops | bytes accessed | tf_op | source)
XLA Modules:
  0.0 348.2 jit_solution(14744054179005626905)
XLA Ops:
  9.8 5.6 %copy.6 = f32[64,128,128]{1,2,0:T(8,128)} copy(f32[64,128,128]{2,1,0:T(8,128)} %param.11) | data formatting | bytes 8388608 | tf_op args[1]
  15.5 6.0 %fusion.61 = f32[64,128,128]{2,1,0:T(8,128)} fusion(f32[64,128,128]{2,1,0:T(8,128)} %param.11, f32[64,128,128]{1,2,0:T(8,128)} %copy.6, pred[64]{0:T(512)(128)(4,1)S(1)} %compare_bitcast_fusion), kind=kLoop, calls=%fused_computation.98 | loop fusion | flops 3145728 | bytes 12582976 | tf_op jit(solution)/shard_map/jit(_where)/select_n | solution.py:92
  22.3 24.5 %while.36 = (s32[]{:T(128)}, f32[4,128,128]{2,0,1:T(4,128)S(1)}, f32[12,128,128]{2,0,1:T(8,128)S(1)}, s32[]{:T(128)}, s32[64]{0:T(128)S(1)}, /*index=5*/s32[]{:T...) while((s32[]{:T(128)}, f32[4,128,128]{2,0,1:T(4,128)S(1)}, ...), condition=%wide.region_1.2_spmd, body=%wide.region_0.1_spmd.sunk | while | flops 428083552 | bytes 8397583 | solution.py:69
  23.7 1.7 fusion.116
  26.9 2.1 fusion.117
  29.0 1.5 convolution_add_fusion.13
  31.8 1.7 fusion.116
  35.1 2.1 fusion.117
  37.2 1.5 convolution_add_fusion.13
  40.0 1.7 fusion.116
  43.3 2.1 fusion.117
  45.3 1.5 convolution_add_fusion.13
  48.3 5.6 %collective-permute-start.2 = (f32[4,128,128]{2,0,1:T(4,128)S(1)}, f32[4,128,128]{2,0,1:T(4,128)S(1)}, u32[]{:S(2)}, u32[]{:S(2)}) collective-permute-start(f32[4,128,128]{2,0,1:T(4,128)S(1)} %get-tuple-element.252), channel_id=1, source_target_pairs={{0,4},{4,8},{8,12},{12,16},{16,20},{20,24},{24,28},{1,5},{5,9},{9,... | collective-permute-start | bytes 786440 | tf_op jit(solution)/shard_map/ppermute | solution.py:34
  54.7 4.6 %collective-permute-done.2 = f32[4,128,128]{2,0,1:T(4,128)S(1)} collective-permute-done((f32[4,128,128]{2,0,1:T(4,128)S(1)}, f32[4,128,128]{2,0,1:T(4,128)S(1)}, u32[]{:S(2)}, u32[]{:S(2)}) %collective-permute-start.2) | collective-permute-done | bytes 262176 | tf_op jit(solution)/shard_map/ppermute | solution.py:34
  62.1 51.8 %collective-permute-done.5 = f32[4,128,128]{2,1,0:T(8,128)S(1)} collective-permute-done((f32[4,128,128]{2,1,0:T(8,128)S(1)}, f32[4,128,128]{2,1,0:T(8,128)S(1)}, u32[]{:S(2)}, u32[]{:S(2)}) %collective-permute-start.5) | collective-permute-done | bytes 262176 | tf_op jit(solution)/shard_map/ppermute | solution.py:34
  114.1 24.5 %while.37 = (s32[]{:T(128)}, f32[4,128,128]{2,0,1:T(4,128)S(1)}, f32[12,128,128]{2,0,1:T(8,128)S(1)}, s32[]{:T(128)}, s32[64]{0:T(128)S(1)}, /*index=5*/s32[]{:T...) while((s32[]{:T(128)}, f32[4,128,128]{2,0,1:T(4,128)S(1)}, ...), condition=%wide.region_3.4_spmd, body=%wide.region_2.3_spmd.sunk | while | flops 428083552 | bytes 8397583 | solution.py:69
  115.5 1.7 fusion.126
  118.7 2.1 fusion.127
  120.8 1.5 convolution_add_fusion.15
  123.6 1.7 fusion.126
  126.9 2.1 fusion.127
  129.0 1.5 convolution_add_fusion.15
  131.8 1.7 fusion.126
  135.1 2.1 fusion.127
  137.1 1.5 convolution_add_fusion.15
  140.1 6.4 %collective-permute-start.6 = (f32[4,128,128]{2,0,1:T(4,128)S(1)}, f32[4,128,128]{2,0,1:T(4,128)S(1)}, u32[]{:S(2)}, u32[]{:S(2)}) collective-permute-start(f32[4,128,128]{2,0,1:T(4,128)S(1)} %get-tuple-element.250), channel_id=1, source_target_pairs={{0,4},{4,8},{8,12},{12,16},{16,20},{20,24},{24,28},{1,5},{5,9},{9,... | collective-permute-start | bytes 786440 | tf_op jit(solution)/shard_map/ppermute | solution.py:34
  146.5 3.8 %collective-permute-done.6 = f32[4,128,128]{2,0,1:T(4,128)S(1)} collective-permute-done((f32[4,128,128]{2,0,1:T(4,128)S(1)}, f32[4,128,128]{2,0,1:T(4,128)S(1)}, u32[]{:S(2)}, u32[]{:S(2)}) %collective-permute-start.6) | collective-permute-done | bytes 262176 | tf_op jit(solution)/shard_map/ppermute | solution.py:34
  153.2 54.4 %collective-permute-done.9 = f32[4,128,128]{2,1,0:T(8,128)S(1)} collective-permute-done((f32[4,128,128]{2,1,0:T(8,128)S(1)}, f32[4,128,128]{2,1,0:T(8,128)S(1)}, u32[]{:S(2)}, u32[]{:S(2)}) %collective-permute-start.9) | collective-permute-done | bytes 262176 | tf_op jit(solution)/shard_map/ppermute | solution.py:34
  207.7 24.7 %while.38 = (s32[]{:T(128)}, f32[4,128,128]{2,0,1:T(4,128)S(1)}, f32[12,128,128]{2,0,1:T(8,128)S(1)}, s32[]{:T(128)}, s32[64]{0:T(128)S(1)}, /*index=5*/s32[]{:T...) while((s32[]{:T(128)}, f32[4,128,128]{2,0,1:T(4,128)S(1)}, ...), condition=%wide.region_5.6_spmd, body=%wide.region_4.5_spmd.sunk | while | flops 428083552 | bytes 8397583 | solution.py:69
  209.3 1.7 fusion.136
  212.5 2.1 fusion.137
  214.6 1.5 convolution_add_fusion.17
  217.5 1.7 fusion.136
  220.7 2.1 fusion.137
  222.8 1.5 convolution_add_fusion.17
  225.6 1.7 fusion.136
  228.9 2.1 fusion.137
  230.9 1.5 convolution_add_fusion.17
  233.9 6.2 %collective-permute-start.10 = (f32[4,128,128]{2,0,1:T(4,128)S(1)}, f32[4,128,128]{2,0,1:T(4,128)S(1)}, u32[]{:S(2)}, u32[]{:S(2)}) collective-permute-start(f32[4,128,128]{2,0,1:T(4,128)S(1)} %get-tuple-element.248), channel_id=1, source_target_pairs={{0,4},{4,8},{8,12},{12,16},{16,20},{20,24},{24,28},{1,5},{5,9},{9,... | collective-permute-start | bytes 786440 | tf_op jit(solution)/shard_map/ppermute | solution.py:34
  240.1 3.8 %collective-permute-done.10 = f32[4,128,128]{2,0,1:T(4,128)S(1)} collective-permute-done((f32[4,128,128]{2,0,1:T(4,128)S(1)}, f32[4,128,128]{2,0,1:T(4,128)S(1)}, u32[]{:S(2)}, u32[]{:S(2)}) %collective-permute-start.10) | collective-permute-done | bytes 262176 | tf_op jit(solution)/shard_map/ppermute | solution.py:34
  244.8 64.1 %all-gather.2.cloned.1.call-done = f32[512,512]{1,0:T(8,128)} async-done(((f32[512,128]{1,0:T(8,128)}), f32[512,512]{1,0:T(8,128)}) %all-gather.2.cloned.1.call-update) | async-done | bytes 1048592 | tf_op jit(solution)/shard_map/all_gather | solution.py:111
  308.9 2.1 convolution_multiply_fusion
  311.0 1.5 collective-permute-start.12
  312.6 7.0 %collective-permute-done.12 = f32[128,512]{1,0:T(8,128)S(1)} collective-permute-done((f32[128,512]{1,0:T(8,128)S(1)}, f32[128,512]{1,0:T(8,128)S(1)}, u32[]{:S(2)}, u32[]{:S(2)}) %collective-permute-start.12) | collective-permute-done | bytes 262176 | tf_op jit(solution)/shard_map/ppermute | solution.py:22
  319.6 1.6 collective-permute-start.13
  321.1 6.1 %collective-permute-done.13 = f32[128,512]{1,0:T(8,128)S(1)} collective-permute-done((f32[128,512]{1,0:T(8,128)S(1)}, f32[128,512]{1,0:T(8,128)S(1)}, u32[]{:S(2)}, u32[]{:S(2)}) %collective-permute-start.13) | collective-permute-done | bytes 262176 | tf_op jit(solution)/shard_map/ppermute | solution.py:22
  327.3 2.5 collective-permute-start.14
  329.7 10.8 %collective-permute-done.14 = f32[128,512]{1,0:T(8,128)S(1)} collective-permute-done((f32[128,512]{1,0:T(8,128)S(1)}, f32[128,512]{1,0:T(8,128)S(1)}, u32[]{:S(2)}, u32[]{:S(2)}) %collective-permute-start.14) | collective-permute-done | bytes 262176 | tf_op jit(solution)/shard_map/ppermute | solution.py:22
  (111 shorter events, 41.2 us)
Async XLA Ops:
  7.2 301.8 %all-gather.2.cloned.1.call-start = ((), (), s32[]{:S(2)}) async-start(), calls=%async_computation | async-start | bytes 1310720 | tf_op jit(solution)/shard_map/all_gather | solution.py:111
  7.2 8.2 %copy-start.1 = (s32[64,2]{0,1:T(2,128)S(1)}, s32[64,2]{0,1:T(2,128)}, u32[]{:S(2)}) copy-start(s32[64,2]{0,1:T(2,128)} %param.12) | copy-start | bytes 1540
  7.2 14.9 %collective-permute-start.1 = (f32[4,128,128]{2,1,0:T(8,128)}, f32[4,128,128]{2,1,0:T(8,128)S(1)}, u32[]{:S(2)}, u32[]{:S(2)}) collective-permute-start(f32[4,128,128]{2,1,0:T(8,128)} %bitcast.89), channel_id=1, source_target_pairs={{8,0},{12,4},{16,8},{20,12},{24,16},{28,20},{9,1},{13,5},{17,9},{2... | collective-permute-start | bytes 786440 | tf_op jit(solution)/shard_map/ppermute | solution.py:34
  8.5 13.6 %collective-permute-start = (f32[4,128,128]{2,1,0:T(8,128)}, f32[4,128,128]{2,1,0:T(8,128)S(1)}, u32[]{:S(2)}, u32[]{:S(2)}) collective-permute-start(f32[4,128,128]{2,1,0:T(8,128)} %bitcast.90), channel_id=1, source_target_pairs={{4,0},{8,4},{12,8},{16,12},{20,16},{24,20},{28,24},{5,1},{9,5},{13... | collective-permute-start | bytes 786440 | tf_op jit(solution)/shard_map/ppermute | solution.py:34
  15.4 6.7 %copy-start = (f32[512,128]{1,0:T(8,128)S(1)}, f32[512,128]{1,0:T(8,128)}, u32[]{:S(2)}) copy-start(f32[512,128]{1,0:T(8,128)} %param.10) | copy-start | bytes 786436
  46.9 7.8 %collective-permute-start.3 = (f32[4,128,128]{2,0,1:T(4,128)S(1)}, f32[4,128,128]{2,0,1:T(4,128)S(1)}, u32[]{:S(2)}, u32[]{:S(2)}) collective-permute-start(f32[4,128,128]{2,0,1:T(4,128)S(1)} %get-tuple-element.253), channel_id=1, source_target_pairs={{0,8},{4,12},{8,16},{12,20},{16,24},{20,28},{1,9},{5,13},{9,17},{1... | collective-permute-start | bytes 786440 | tf_op jit(solution)/shard_map/ppermute | solution.py:34
  48.3 11.1 %collective-permute-start.2 = (f32[4,128,128]{2,0,1:T(4,128)S(1)}, f32[4,128,128]{2,0,1:T(4,128)S(1)}, u32[]{:S(2)}, u32[]{:S(2)}) collective-permute-start(f32[4,128,128]{2,0,1:T(4,128)S(1)} %get-tuple-element.252), channel_id=1, source_target_pairs={{0,4},{4,8},{8,12},{12,16},{16,20},{20,24},{24,28},{1,5},{5,9},{9,... | collective-permute-start | bytes 786440 | tf_op jit(solution)/shard_map/ppermute | solution.py:34
  59.5 54.4 %collective-permute-start.5 = (f32[4,128,128]{2,1,0:T(8,128)S(1)}, f32[4,128,128]{2,1,0:T(8,128)S(1)}, u32[]{:S(2)}, u32[]{:S(2)}) collective-permute-start(f32[4,128,128]{2,1,0:T(8,128)S(1)} %bitcast.83), channel_id=1, source_target_pairs={{8,0},{12,4},{16,8},{20,12},{24,16},{28,20},{9,1},{13,5},{17,9},{2... | collective-permute-start | bytes 786440 | tf_op jit(solution)/shard_map/ppermute | solution.py:34
  60.8 53.1 %collective-permute-start.4 = (f32[4,128,128]{2,1,0:T(8,128)S(1)}, f32[4,128,128]{2,1,0:T(8,128)S(1)}, u32[]{:S(2)}, u32[]{:S(2)}) collective-permute-start(f32[4,128,128]{2,1,0:T(8,128)S(1)} %bitcast.84), channel_id=1, source_target_pairs={{4,0},{8,4},{12,8},{16,12},{20,16},{24,20},{28,24},{5,1},{9,5},{13... | collective-permute-start | bytes 786440 | tf_op jit(solution)/shard_map/ppermute | solution.py:34
  138.7 7.8 %collective-permute-start.7 = (f32[4,128,128]{2,0,1:T(4,128)S(1)}, f32[4,128,128]{2,0,1:T(4,128)S(1)}, u32[]{:S(2)}, u32[]{:S(2)}) collective-permute-start(f32[4,128,128]{2,0,1:T(4,128)S(1)} %get-tuple-element.251), channel_id=1, source_target_pairs={{0,8},{4,12},{8,16},{12,20},{16,24},{20,28},{1,9},{5,13},{9,17},{1... | collective-permute-start | bytes 786440 | tf_op jit(solution)/shard_map/ppermute | solution.py:34
  140.1 10.3 %collective-permute-start.6 = (f32[4,128,128]{2,0,1:T(4,128)S(1)}, f32[4,128,128]{2,0,1:T(4,128)S(1)}, u32[]{:S(2)}, u32[]{:S(2)}) collective-permute-start(f32[4,128,128]{2,0,1:T(4,128)S(1)} %get-tuple-element.250), channel_id=1, source_target_pairs={{0,4},{4,8},{8,12},{12,16},{16,20},{20,24},{24,28},{1,5},{5,9},{9,... | collective-permute-start | bytes 786440 | tf_op jit(solution)/shard_map/ppermute | solution.py:34
  150.6 57.0 %collective-permute-start.9 = (f32[4,128,128]{2,1,0:T(8,128)S(1)}, f32[4,128,128]{2,1,0:T(8,128)S(1)}, u32[]{:S(2)}, u32[]{:S(2)}) collective-permute-start(f32[4,128,128]{2,1,0:T(8,128)S(1)} %bitcast.95), channel_id=1, source_target_pairs={{8,0},{12,4},{16,8},{20,12},{24,16},{28,20},{9,1},{13,5},{17,9},{2... | collective-permute-start | bytes 786440 | tf_op jit(solution)/shard_map/ppermute | solution.py:34
  151.9 55.7 %collective-permute-start.8 = (f32[4,128,128]{2,1,0:T(8,128)S(1)}, f32[4,128,128]{2,1,0:T(8,128)S(1)}, u32[]{:S(2)}, u32[]{:S(2)}) collective-permute-start(f32[4,128,128]{2,1,0:T(8,128)S(1)} %bitcast.96), channel_id=1, source_target_pairs={{4,0},{8,4},{12,8},{16,12},{20,16},{24,20},{28,24},{5,1},{9,5},{13... | collective-permute-start | bytes 786440 | tf_op jit(solution)/shard_map/ppermute | solution.py:34
  232.6 7.5 %collective-permute-start.11 = (f32[4,128,128]{2,0,1:T(4,128)S(1)}, f32[4,128,128]{2,0,1:T(4,128)S(1)}, u32[]{:S(2)}, u32[]{:S(2)}) collective-permute-start(f32[4,128,128]{2,0,1:T(4,128)S(1)} %get-tuple-element.249), channel_id=1, source_target_pairs={{0,8},{4,12},{8,16},{12,20},{16,24},{20,28},{1,9},{5,13},{9,17},{1... | collective-permute-start | bytes 786440 | tf_op jit(solution)/shard_map/ppermute | solution.py:34
  233.9 10.1 %collective-permute-start.10 = (f32[4,128,128]{2,0,1:T(4,128)S(1)}, f32[4,128,128]{2,0,1:T(4,128)S(1)}, u32[]{:S(2)}, u32[]{:S(2)}) collective-permute-start(f32[4,128,128]{2,0,1:T(4,128)S(1)} %get-tuple-element.248), channel_id=1, source_target_pairs={{0,4},{4,8},{8,12},{12,16},{16,20},{20,24},{24,28},{1,5},{5,9},{9,... | collective-permute-start | bytes 786440 | tf_op jit(solution)/shard_map/ppermute | solution.py:34
  311.0 8.5 %collective-permute-start.12 = (f32[128,512]{1,0:T(8,128)S(1)}, f32[128,512]{1,0:T(8,128)S(1)}, u32[]{:S(2)}, u32[]{:S(2)}) collective-permute-start(f32[128,512]{1,0:T(8,128)S(1)} %convolution_multiply_fusion), channel_id=1, source_target_pairs={{0,4},{4,0},{8,12},{12,8},{16,20},{20,16},{24,28},{28,24},{1,5},{5... | collective-permute-start | bytes 786440 | tf_op jit(solution)/shard_map/ppermute | solution.py:22
  319.6 7.7 %collective-permute-start.13 = (f32[128,512]{1,0:T(8,128)S(1)}, f32[128,512]{1,0:T(8,128)S(1)}, u32[]{:S(2)}, u32[]{:S(2)}) collective-permute-start(f32[128,512]{1,0:T(8,128)S(1)} %add.146), channel_id=1, source_target_pairs={{0,8},{4,12},{8,0},{12,4},{16,24},{20,28},{24,16},{28,20},{1,9},{5... | collective-permute-start | bytes 786440 | tf_op jit(solution)/shard_map/ppermute | solution.py:22
  327.3 13.3 %collective-permute-start.14 = (f32[128,512]{1,0:T(8,128)S(1)}, f32[128,512]{1,0:T(8,128)S(1)}, u32[]{:S(2)}, u32[]{:S(2)}) collective-permute-start(f32[128,512]{1,0:T(8,128)S(1)} %add.147), channel_id=1, source_target_pairs={{0,16},{4,20},{8,24},{12,28},{16,0},{20,4},{24,8},{28,12},{1,17},{... | collective-permute-start | bytes 786440 | tf_op jit(solution)/shard_map/ppermute | solution.py:22
Sparse Core Ops, SparseCore 0:
  244.9 63.9 all-gather.1
